TPU v7x, 512 devices: a whole 4x8x8 slice. The times are simulated.
512 devices in a mesh: seq: 128 (over y, z, core), head: 4 (over x).
Axes of the slice: x: 4, y: 8, z: 8, core: 2. Of those that a mesh axis runs over, the one named last changes fastest.
Arguments:
- tokens: bfloat16 [16384, 2048], P('seq', 'head'), as said below
- w_query: bfloat16 [2048, 1024], P(None, 'head'), may hold values from -0.125 to 0.125
- w_key: bfloat16 [2048, 1024], P(None, 'head')
- w_value: bfloat16 [2048, 1024], P(None, 'head'), may hold values from -0.125 to 0.125
- gate_codes: int32 [16384, 8], P('seq', 'head'), may hold values from 28 to 1572854, as said below
- beta_codes: int32 [16384, 8], P('seq', 'head'), may hold values from 32 to 256
- norm_gain: float32 [128], replicated, may hold values from 0.25 to 1.75
- w_out: bfloat16 [1024, 2048], P('head'), may hold values from -0.1875 to 0.1875
Outputs:
- mixed: bfloat16 [16384, 2048], P('seq', 'head')
Inputs may be any that keep to these rules, and one draw needn't show every extreme that they name: `gate_codes`: codes are positive; the sweep's gates are those of one recording, identical law in every draw. `tokens`: activations of order one to ten.
All inputs are finite; a program needn't handle non-finite values.
Results may differ from a plain program's by a relative error of at most 0.0049.
Values may be sent and summed in bfloat16 or wider, within the bound.
A program may use at most 128 MiB of HBM per device.

v0:
```python
import jax
import jax.numpy as jnp
from jax import lax
from jax.sharding import PartitionSpec as P

SPAN = 64


def entering(part, axis, combine, identity):
    place = lax.axis_index(axis)
    gathered = jax.tree.map(lambda a: lax.all_gather(a, axis), part)
    state = jax.tree.map(lambda a, e: jnp.zeros_like(a) + jnp.asarray(e, a.dtype), part, identity)

    def one(step, state):
        return combine(
            state, jax.tree.map(lambda a: lax.dynamic_index_in_dim(a, step, 0, False), gathered)
        )

    return lax.fori_loop(0, place, one, state)


def shards(tokens, w_query, w_key, w_value, gate_codes, beta_codes, norm_gain, w_out):
    highest = lax.Precision.HIGHEST
    tok_rows = tokens.shape[0]
    heads_here = gate_codes.shape[1]
    head_size = norm_gain.shape[0]
    n_spans = tok_rows // SPAN
    piece = lax.all_gather(tokens, "head", axis=1, tiled=True)
    query, key_rows, value = tuple(
        (
            jnp.dot(piece, weight, preferred_element_type=jnp.float32)
            for weight in (w_query, w_key, w_value)
        )
    )

    def split_heads(array):
        return array.reshape(n_spans, SPAN, heads_here, head_size).transpose(2, 0, 1, 3)

    queries = split_heads(query)
    unit_keys = split_heads(key_rows)
    unit_keys = unit_keys * lax.rsqrt(jnp.sum(unit_keys * unit_keys, -1, keepdims=True) + 1e-06)
    values = split_heads(value)
    decay_log = (
        (-gate_codes.astype(jnp.float32) / 2097152.0)
        .reshape(n_spans, SPAN, heads_here)
        .transpose(2, 0, 1)
    )
    log_decay = jnp.cumsum(decay_log, axis=-1)
    betas = (
        (beta_codes.astype(jnp.float32) / 256.0)
        .reshape(n_spans, SPAN, heads_here)
        .transpose(2, 0, 1)
    )
    positions = jnp.arange(SPAN)
    lower_incl = positions[:, None] >= positions[None, :]
    lower_strict = positions[:, None] > positions[None, :]
    gaps = log_decay[..., :, None] - log_decay[..., None, :]
    inclusive = jnp.where(lower_incl, jnp.exp(jnp.where(lower_incl, gaps, 0.0)), 0.0)
    strict = jnp.where(lower_strict, inclusive, 0.0)
    key_dots = jnp.einsum("hctd,hcid->hcti", unit_keys, unit_keys, precision=highest)
    system = jnp.eye(SPAN, dtype=jnp.float32) + betas[..., :, None] * key_dots * strict
    right = jnp.concatenate(
        [betas[..., None] * unit_keys * jnp.exp(log_decay)[..., None], betas[..., None] * values],
        axis=-1,
    )
    solved = jax.scipy.linalg.solve_triangular(system, right, lower=True, unit_diagonal=True)
    wy_keys = solved[..., :head_size]
    wy_values = solved[..., head_size:]
    query_dots = jnp.einsum("hctd,hcid->hcti", queries, unit_keys, precision=highest) * inclusive
    intra = jnp.einsum("hcti,hciv->hctv", query_dots, wy_values, precision=highest)
    query_eff = queries * jnp.exp(log_decay)[..., None] - jnp.einsum(
        "hcti,hcik->hctk", query_dots, wy_keys, precision=highest
    )
    last_log = log_decay[..., -1]
    key_tail = unit_keys * jnp.exp(last_log[..., None] - log_decay)[..., None]
    identity_mat = jnp.eye(head_size, dtype=jnp.float32)
    span_maps = jnp.exp(last_log)[..., None, None] * identity_mat - jnp.einsum(
        "hctk,hctj->hckj", wy_keys, key_tail, precision=highest
    )
    span_adds = jnp.einsum("hctv,hctk->hcvk", wy_values, key_tail, precision=highest)
    span_maps = jnp.moveaxis(span_maps, 1, 0)
    span_adds = jnp.moveaxis(span_adds, 1, 0)
    zero_state = jnp.zeros((heads_here, head_size, head_size), jnp.float32)
    unit_maps = jnp.broadcast_to(identity_mat, (heads_here, head_size, head_size))

    def advance(carry, inputs):
        state, product = carry
        step_map, step_add = inputs
        new_state = jnp.einsum("hvk,hkj->hvj", state, step_map, precision=highest) + step_add
        new_product = jnp.einsum("hik,hkj->hij", product, step_map, precision=highest)
        return ((new_state, new_product), (state, product))

    def summarize(carry, inputs):
        new_carry, _ = advance(carry, inputs)
        return (new_carry, None)

    def combine(earlier, later):
        return (
            jnp.einsum("hik,hkj->hij", earlier[0], later[0], precision=highest),
            jnp.einsum("hvk,hkj->hvj", earlier[1], later[0], precision=highest) + later[1],
        )

    (summary_state, summary_map), _ = lax.scan(
        summarize, (zero_state, unit_maps), (span_maps, span_adds)
    )
    _, incoming = entering((summary_map, summary_state), "seq", combine, (unit_maps, zero_state))

    def replay(state, inputs):
        step_map, step_add = inputs
        return (jnp.einsum("hvk,hkj->hvj", state, step_map, precision=highest) + step_add, state)

    _, starts = lax.scan(replay, incoming, (span_maps, span_adds))
    outputs = intra + jnp.einsum("hctk,chvk->hctv", query_eff, starts, precision=highest)
    normed = outputs * lax.rsqrt(jnp.mean(outputs * outputs, -1, keepdims=True) + 1e-06) * norm_gain
    normed = (
        normed.astype(jnp.bfloat16).transpose(1, 2, 0, 3).reshape(tok_rows, heads_here * head_size)
    )
    partial_out = jnp.dot(normed, w_out, preferred_element_type=jnp.float32)
    return lax.psum_scatter(partial_out, "head", scatter_dimension=1, tiled=True).astype(
        jnp.bfloat16
    )


def solution(mesh):
    return jax.shard_map(
        shards,
        mesh=mesh,
        in_specs=(
            P("seq", "head"),
            P(None, "head"),
            P(None, "head"),
            P(None, "head"),
            P("seq", "head"),
            P("seq", "head"),
            P(),
            P("head", None),
        ),
        out_specs=P("seq", "head"),
        check_vma=False,
    )
```

profile of v0, /device:TPU:1, one launch (start us, length us, event | category | flops | bytes accessed | tf_op | source)
XLA Modules:
  0.0 590.5 jit_solution(8923890875720144227)
XLA Ops:
  6.5 0.0 copy-start
  6.5 0.0 all-gather.5.cloned.1.call-start
  6.6 0.8 negate_multiply_fusion
  7.4 0.1 reshape.72
  7.5 0.0 copy-start.1
  7.5 0.5 reduce_window_sum.11
  7.9 0.2 slice_reduce_fusion
  8.1 0.1 subtract_exponential_fusion
  8.2 11.3 %all_gather.15 = bf16[128,2048]{1,0:T(8,128)(2,1)S(1)} all-gather(bf16[128,512]{1,0:T(8,128)(2,1)} %param.14), channel_id=1, replica_groups=mesh['seq'=128,'head'=4] {'head'}, dimensions={1}, use_global_device_ids=true | all-gather | bytes 655360 | tf_op jit(solution)/shard_map/all_gather | solution.py:28
  19.4 1.5 fusion.56
  21.0 0.1 reshape.71
  21.1 0.1 fusion.32
  21.2 0.7 convert_multiply_fusion
  21.9 0.1 reshape.73
  22.0 1.5 fusion.57
  23.5 0.1 reshape.74
  23.6 0.1 iota_compare_fusion.2
  23.7 0.4 fusion.24
  24.1 19.7 %custom-call.4 = f32[2,2,1,64,64]{3,4,2,1,0:T(8,128)S(1)} custom-call(f32[2,2,1,64,64]{4,3,2,1,0:T(8,128)S(1)} %fusion.24), custom_call_target="InvertDiagBlocksLowerTriangular" | custom-call | tf_op jit(solution)/shard_map/jit(_solve_triangular)/vmap(vmap())/triangular_solve | solution.py:66
  43.8 0.1 copy.46
  43.9 0.2 multiply_multiply_fusion
  44.1 0.4 fusion.25
  44.5 0.7 convolution_bitcast_fusion.4
  45.2 0.7 fusion.19
  45.9 0.1 copy.47
  46.0 0.1 copy.48
  46.2 1.2 while.39
  46.2 0.3 fusion.93
  46.5 0.3 convolution_bitcast_fusion.7
  46.8 0.3 fusion.93
  47.1 0.3 convolution_bitcast_fusion.7
  47.4 0.8 copy.49
  48.1 0.0 all-gather.5.cloned.1.call-update
  48.2 0.0 all-gather.7.cloned.1.call-start
  48.2 0.7 copy.50
  49.0 0.0 all-gather.7.cloned.1.call-update
  49.0 0.0 reduce-scatter.2.cloned.1.call-start
  49.1 1.5 fusion.55
  50.6 0.1 reshape.70
  50.7 0.4 convolution_multiply_fusion.1
  51.1 0.3 fusion.37
  51.4 0.3 convolution_subtract_fusion
  51.6 104.8 %all-gather.5.cloned.1.call-done = f32[256,128,128]{2,1,0:T(8,128)} async-done(((f32[2,128,128]{2,1,0:T(8,128)}), f32[256,128,128]{2,1,0:T(8,128)}) %all-gather.5.cloned.1.call-update) | async-done | bytes 16777232 | tf_op jit(solution)/shard_map/all_gather | solution.py:11
  156.4 101.3 %all-gather.7.cloned.1.call-done = f32[256,128,128]{2,1,0:T(8,128)} async-done(((f32[2,128,128]{2,1,0:T(8,128)}), f32[256,128,128]{2,1,0:T(8,128)}) %all-gather.7.cloned.1.call-update) | async-done | bytes 16777232 | tf_op jit(solution)/shard_map/all_gather | solution.py:11
  257.7 2.4 while.37
  257.8 0.9 constant_dynamic-slice_fusion.2
  258.7 0.1 copy.95
  258.8 1.3 fusion.85
  260.1 0.7 while.38
  260.2 0.3 fusion.88
  260.5 0.3 fusion.88
  260.8 0.5 multiply_reduce_fusion
  261.3 0.0 copy-done.1
  261.3 0.1 fusion.30
  261.4 0.1 copy.56
  261.5 0.0 copy-done
  261.5 1.3 fusion.42
  262.7 0.0 reduce-scatter.2.cloned.1.call-update
  262.8 319.6 %reduce-scatter.2.cloned.1.call-done = f32[128,512]{1,0:T(8,128)} async-done(((f32[128,2048]{1,0:T(8,128)}), f32[128,512]{1,0:T(8,128)}) %reduce-scatter.2.cloned.1.call-update) | async-done | bytes 262160 | tf_op jit(solution)/shard_map/reduce_scatter | solution.py:119
  582.4 1.6 convert_element_type.34
  (20 shorter events, 0.2 us)
Async XLA Ops:
  6.5 254.9 %copy-start = (bf16[256,2048]{1,0:T(8,128)(2,1)S(1)}, bf16[256,2048]{1,0:T(8,128)(2,1)}, u32[]{:S(2)}) copy-start(bf16[256,2048]{1,0:T(8,128)(2,1)} %param.21) | copy-start | bytes 3145732
  6.5 149.9 %all-gather.5.cloned.1.call-start = ((), (), s32[]{:S(2)}) async-start(), calls=%async_computation.2 | async-start | bytes 16908288 | tf_op jit(solution)/shard_map/all_gather | solution.py:11
  7.5 253.8 %copy-start.1 = (f32[128]{0:T(128)S(1)}, f32[128]{0:T(128)}, u32[]{:S(2)}) copy-start(f32[128]{0:T(128)} %param.20) | copy-start | bytes 1540
  48.2 209.6 %all-gather.7.cloned.1.call-start = ((), (), s32[]{:S(2)}) async-start(), calls=%async_computation.3 | async-start | bytes 16908288 | tf_op jit(solution)/shard_map/all_gather | solution.py:11
  49.0 533.4 %reduce-scatter.2.cloned.1.call-start = ((), (), s32[]{:S(2)}) async-start(), calls=%async_computation.1 | async-start | bytes 1310720 | tf_op jit(solution)/shard_map/reduce_scatter | solution.py:119
Sparse Core Ops, SparseCore 0:
  48.3 108.0 all-gather.4
  159.5 98.1 all-gather.6
  262.9 319.4 reduce-scatter.1
where the time goes:
time: 596 us; the launch traced here: 591 us
  waiting for transfers between devices  526 us (88%)
  other arithmetic  23.8 us (4%)
  between operations  13.4 us (2%)
  matrix products  12.4 us (2%)
  blocking collectives  11.3 us (2%)
    reduce_scatter x1, waiting for transfers between devices, shards(): lax.psum_scatter(partial_out, 'head', scatter_dimension=1, tiled=True)  320 us
    all_gather x2, waiting for transfers between devices, entering(): gathered = jax.tree.map(lambda a: lax.all_gather(a, axis), part)  206 us
    another operation x3, other arithmetic, shards(): jax.scipy.linalg.solve_triangular(system, right, lower=True, unit_diagona...  19.7 us
  transfers between devices with their start and end apart: 3, of which 3 were waited for; matrix products, arithmetic and copies ran while one was open for 1% of the time, Pallas kernels for 0%

commit v1 on v0

v1 whole, which is shorter than its diff:
```python
import functools
import jax
import jax.numpy as jnp
from jax import lax
from jax.experimental import pallas as pl
from jax.experimental.pallas import tpu as pltpu
from jax.sharding import PartitionSpec as P

MESH = pl.DeviceIdType.MESH
WIRE = jnp.bfloat16
F32 = jnp.float32
BF16 = jnp.bfloat16


def mm(a, b, dims=((1,), (0,))):
    return lax.dot_general(a, b, (dims, ((), ())), preferred_element_type=F32)


def halves(a):
    high = a.astype(BF16)
    return high, (a - high.astype(F32)).astype(BF16)


def dot3(a, b, dims=((1,), (0,))):
    a_high, a_low = halves(a)
    b_high, b_low = halves(b)
    return mm(a_high, b_high, dims) + (mm(a_high, b_low, dims) + mm(a_low, b_high, dims))


def dot2(a, b):
    a_high, a_low = halves(a)
    return mm(a_high, b) + mm(a_low, b)


def by_map(a, b):
    return dot2(a, b) if b.dtype == BF16 else dot3(a, b)


def below(top, rows):
    return jnp.concatenate([jnp.zeros((top, rows.shape[1]), F32), rows.astype(F32)], axis=0)


def unit_inverse(low, rows, cols):
    size = low.shape[0]
    eye = (rows == cols).astype(F32)
    base = jnp.where(rows // 8 == cols // 8, low, 0.0)
    square = dot3(base, base)
    fourth = dot3(square, square)
    result = dot3(dot3(eye - base, eye + square), eye + fourth)
    width = 8
    while width < size:
        mask = (rows // (2 * width) == cols // (2 * width)) & (rows // width > cols // width)
        corner = jnp.where(mask, low, 0.0)
        result = result - dot3(dot3(result, corner), result)
        width *= 2
    return result


def kernel(
    nx, ny, nz,
    tok_ref, wq_hbm, wk_hbm, wv_hbm, gate_ref, beta_ref, gain_ref, wo_hbm,
    out_ref,
    tok_all, wq, wk, wv, wo_all, ex_send, ex_recv, gz, gy, st_send, st_recv, norm_all, eff, intra,
    load_sem, x_send, x_recv, wo_send, wo_recv, n_send, n_recv, core_send, core_recv,
    z_send, z_recv, y_send, y_recv,
):
    index = lax.axis_index("seq")
    x = lax.axis_index("head")
    core = index % 2
    z = (index // 2) % nz
    y = index // (2 * nz)
    size = gain_ref.shape[1]
    n_tok, width = tok_ref.shape
    out_cols = out_ref.shape[1]

    def at(y_to, z_to, core_to, x_to):
        return ((y_to * nz + z_to) * 2 + core_to, x_to)

    x_right, x_left = at(y, z, core, (x + 1) % nx), at(y, z, core, (x + nx - 1) % nx)
    z_right, z_left = at(y, (z + 1) % nz, core, x), at(y, (z + nz - 1) % nz, core, x)
    y_right, y_left = at((y + 1) % ny, z, core, x), at((y + ny - 1) % ny, z, core, x)
    partner = at(y, z, 1 - core, x)

    loads = [
        pltpu.make_async_copy(source, target, load_sem.at[i])
        for i, (source, target) in enumerate(((wq_hbm, wq), (wk_hbm, wk), (wv_hbm, wv)))
    ]
    for load in loads:
        load.start()
    own_cols = pl.ds(pl.multiple_of(x * out_cols, 128), out_cols)
    own_out = pltpu.make_async_copy(wo_hbm.at[:, own_cols], wo_all.at[x], load_sem.at[3])
    own_out.start()

    friends = [at(y, z, core, (x + d) % nx) for d in range(1, nx)]
    friends += [partner]
    friends += [z_right] + ([z_left] if nz > 2 else [])
    friends += [y_right] + ([y_left] if ny > 2 else [])
    barrier = pltpu.get_barrier_semaphore()
    for friend in friends:
        pl.semaphore_signal(barrier, inc=1, device_id=friend, device_id_type=MESH)
    pl.semaphore_wait(barrier, len(friends))

    def send(source, target, s_sem, r_sem, to):
        return pltpu.make_async_remote_copy(
            src_ref=source, dst_ref=target, send_sem=s_sem, recv_sem=r_sem,
            device_id=to, device_id_type=MESH,
        )

    def x_gather(own, slots, s_sems, r_sems, use):
        half = own.shape[0] // 2
        before, after, across = (x + nx - 1) % nx, (x + 1) % nx, (x + 2) % nx
        first = send(own, slots.at[x], s_sems.at[0], r_sems.at[0], x_right)
        second = send(own, slots.at[x], s_sems.at[1], r_sems.at[1], x_left)
        first.start()
        second.start()
        use(x, own[...])
        first.wait_recv()
        top = slots.at[before, pl.ds(0, half)]
        third = send(top, top, s_sems.at[2], r_sems.at[2], x_right)
        third.start()
        second.wait_recv()
        low = slots.at[after, pl.ds(half, half)]
        fourth = send(low, low, s_sems.at[3], r_sems.at[3], x_left)
        fourth.start()
        use(before, slots[before])
        use(after, slots[after])
        third.wait_recv()
        fourth.wait_recv()
        use(across, slots[across])
        for copy in (first, second, third, fourth):
            copy.wait_send()

    sums = [jnp.zeros((n_tok, wq.shape[1]), F32) for _ in range(3)]
    loaded = []

    def project(place, block):
        if not loaded:
            for load in loads:
                load.wait()
            loaded.append(True)
        part = pl.ds(pl.multiple_of(place * width, 128), width)
        for i, weight in enumerate((wq, wk, wv)):
            sums[i] = sums[i] + mm(block, weight[part, :])

    x_gather(tok_ref, tok_all, x_send, x_recv, project)

    own_out.wait()
    out_copies = []
    for d in range(1, nx):
        there = (x + d) % nx
        cols = pl.ds(pl.multiple_of(there * out_cols, 128), out_cols)
        out_copies.append(
            send(wo_hbm.at[:, cols], wo_all.at[x], wo_send.at[d - 1], wo_recv.at[d - 1],
                 at(y, z, core, there))
        )
    for copy in out_copies:
        copy.start()

    rows = lax.broadcasted_iota(jnp.int32, (n_tok, n_tok), 0)
    cols = lax.broadcasted_iota(jnp.int32, (n_tok, n_tok), 1)
    lower = rows >= cols
    ones_low = lower.astype(BF16)
    maps = []
    for head in range(2):
        cut = slice(head * size, (head + 1) * size)
        query, key, value = (s[:, cut] for s in sums)
        key = key * lax.rsqrt(jnp.sum(key * key, -1, keepdims=True) + 1e-06)
        code = -gate_ref[:, head : head + 1].astype(F32) / 2097152.0
        beta = beta_ref[:, head : head + 1].astype(F32) / 256.0
        spread = jnp.broadcast_to(code, (n_tok, n_tok))
        c_high, c_low = halves(spread)
        c_last = (spread - c_high.astype(F32) - c_low.astype(F32)).astype(BF16)
        logs = mm(ones_low, c_high) + (mm(ones_low, c_low) + mm(ones_low, c_last))
        gaps = logs - logs.T
        incl = jnp.where(lower, jnp.exp(jnp.where(lower, gaps, 0.0)), 0.0)
        strict = jnp.where(rows > cols, incl, 0.0)
        log = logs[:, 0:1]
        last = logs[n_tok - 1 : n_tok, 0:1]
        low = beta * dot3(key, key, ((1,), (1,))) * strict
        inverse = unit_inverse(low, rows, cols)
        right = jnp.concatenate([beta * key * jnp.exp(log), beta * value], axis=1)
        solved = dot3(inverse, right)
        dots = dot3(query, key, ((1,), (1,))) * incl
        inner = dot3(dots, solved)
        intra[head] = inner[:, size:]
        eff[head] = query * jnp.exp(log) - inner[:, :size]
        tail = key * jnp.exp(last - log)
        signed = jnp.concatenate([-solved[:, :size], solved[:, size:]], axis=1)
        moved = dot3(signed, tail, ((0,), (0,)))
        r2 = lax.broadcasted_iota(jnp.int32, (2 * size, size), 0)
        c2 = lax.broadcasted_iota(jnp.int32, (2 * size, size), 1)
        maps.append(moved + jnp.where(r2 == c2, jnp.exp(last), 0.0))

    first_core = core == 0
    ex_send[...] = jnp.where(first_core, maps[1], maps[0])
    swap = send(ex_send, ex_recv, core_send.at[0], core_recv.at[0], partner)
    swap.start()
    mine = jnp.where(first_core, maps[0], maps[1])
    swap.wait_recv()
    other = ex_recv[...]
    early = jnp.where(first_core, mine, other)
    late = jnp.where(first_core, other, mine)
    gz[z] = (dot3(early, late[:size]) + below(size, late[size:])).astype(WIRE)

    def ring(slots, place, count, s_sems, r_sems, right_id, left_id):
        ahead, behind = count // 2, count - 1 - count // 2
        started = []
        rights, lefts = [], []
        for step in range(max(ahead, behind)):
            if step < ahead:
                slot = (place + count - step) % count
                if step:
                    rights[-1].wait_recv()
                copy = send(slots.at[slot], slots.at[slot], s_sems.at[0, step], r_sems.at[0, step], right_id)
                copy.start()
                rights.append(copy)
            if step < behind:
                slot = (place + step) % count
                if step:
                    lefts[-1].wait_recv()
                copy = send(slots.at[slot], slots.at[slot], s_sems.at[1, step], r_sems.at[1, step], left_id)
                copy.start()
                lefts.append(copy)
        for copies in (rights, lefts):
            if copies:
                copies[-1].wait_recv()
            started += copies
        return started

    z_copies = ring(gz, z, nz, z_send, z_recv, z_right, z_left)
    total = gz[0].astype(F32)
    r2 = lax.broadcasted_iota(jnp.int32, (2 * size, size), 0)
    c2 = lax.broadcasted_iota(jnp.int32, (2 * size, size), 1)
    prefix = (r2 == c2).astype(F32)
    for j in range(1, nz):
        prefix = jnp.where(z == j, total, prefix)
        nxt = gz[j]
        total = by_map(total, nxt[:size]) + below(size, nxt[size:])
    gy[y] = total.astype(WIRE)
    y_copies = ring(gy, y, ny, y_send, y_recv, y_right, y_left)
    state = jnp.zeros((size, size), F32)
    for j in range(ny - 1):
        nxt = gy[j]
        state = jnp.where(y > j, by_map(state, nxt[:size]) + nxt[size:].astype(F32), state)
    chip = dot3(state, prefix[:size]) + prefix[size:]
    second = dot3(chip, early[:size]) + early[size:]
    st_send[...] = jnp.where(first_core, second, chip)
    give = send(st_send, st_recv, core_send.at[1], core_recv.at[1], partner)
    give.start()
    kept = jnp.where(first_core, chip, second)
    give.wait_recv()
    got = st_recv[...]
    states = [jnp.where(first_core, kept, got), jnp.where(first_core, got, kept)]
    gain = gain_ref[...]
    for head in range(2):
        o = intra[head] + dot3(eff[head], states[head], ((1,), (1,)))
        scale = lax.rsqrt(jnp.mean(o * o, -1, keepdims=True) + 1e-06)
        norm_all[x, :, head * size : (head + 1) * size] = (o * scale * gain).astype(BF16)

    result = [jnp.zeros((n_tok, out_cols), F32)]
    arrived = []

    def finish(place, block):
        if len(arrived) == 1:
            for copy in out_copies:
                copy.wait_recv()
        arrived.append(True)
        result[0] = result[0] + mm(block, wo_all[place])

    x_gather(norm_all.at[x], norm_all, n_send, n_recv, finish)
    out_ref[...] = result[0].astype(BF16)
    for copy in out_copies + z_copies + y_copies + [swap, give]:
        copy.wait_send()


def shards(ny, nz, nx, tokens, w_query, w_key, w_value, gate_codes, beta_codes, norm_gain, w_out):
    n_tok, width = tokens.shape
    size = norm_gain.shape[0]
    here = w_query.shape[1]
    vmem = pl.BlockSpec(memory_space=pltpu.VMEM)
    hbm = pl.BlockSpec(memory_space=pl.ANY)
    dma = pltpu.SemaphoreType.DMA
    return pl.pallas_call(
        functools.partial(kernel, nx, ny, nz),
        out_shape=jax.ShapeDtypeStruct((n_tok, w_out.shape[1] // nx), BF16),
        in_specs=[vmem, hbm, hbm, hbm, vmem, vmem, vmem, hbm],
        out_specs=vmem,
        scratch_shapes=[
            pltpu.VMEM((nx, n_tok, width), BF16),
            pltpu.VMEM(w_query.shape, BF16),
            pltpu.VMEM(w_key.shape, BF16),
            pltpu.VMEM(w_value.shape, BF16),
            pltpu.VMEM((nx, here, w_out.shape[1] // nx), BF16),
            pltpu.VMEM((2 * size, size), F32),
            pltpu.VMEM((2 * size, size), F32),
            pltpu.VMEM((nz, 2 * size, size), WIRE),
            pltpu.VMEM((ny, 2 * size, size), WIRE),
            pltpu.VMEM((size, size), F32),
            pltpu.VMEM((size, size), F32),
            pltpu.VMEM((nx, n_tok, here), BF16),
            pltpu.VMEM((2, n_tok, size), F32),
            pltpu.VMEM((2, n_tok, size), F32),
            dma((4,)), dma((4,)), dma((4,)), dma((nx - 1,)), dma((nx - 1,)), dma((4,)), dma((4,)),
            dma((2,)), dma((2,)), dma((2, nz)), dma((2, nz)), dma((2, ny)), dma((2, ny)),
        ],
        compiler_params=pltpu.CompilerParams(
            collective_id=0, has_side_effects=True, vmem_limit_bytes=40 << 20
        ),
    )(tokens, w_query, w_key, w_value, gate_codes, beta_codes, norm_gain.reshape(1, size), w_out)


def solution(mesh):
    chips = mesh.shape["seq"] // 2
    nz = 1
    while nz * nz < chips:
        nz *= 2
    return jax.shard_map(
        functools.partial(shards, chips // nz, nz, mesh.shape["head"]),
        mesh=mesh,
        in_specs=(
            P("seq", "head"), P(None, "head"), P(None, "head"), P(None, "head"),
            P("seq", "head"), P("seq", "head"), P(), P("head", None),
        ),
        out_specs=P("seq", "head"),
        check_vma=False,
    )
```

time: 596 us -> 74.7 us (0.13)
  waiting for transfers between devices: 526 us -> 0 us
  Pallas kernels: 0 us -> 67.2 us
  other arithmetic: 23.8 us -> 0 us
  between operations: 13.4 us -> 0.04 us
  matrix products: 12.4 us -> 0 us
  blocking collectives: 11.3 us -> 0 us
    reduce_scatter x1 -> x0, waiting for transfers between devices: 320 us -> none  [shards(): lax.psum_scatter(partial_out, 'head', scatter_dimension=1, tiled=True)]
    all_gather x2 -> x0, waiting for transfers between devices: 206 us -> none  [entering(): gathered = jax.tree.map(lambda a: lax.all_gather(a, axis), part)]
    pallas_call x0 -> x1, Pallas kernels: none -> 67.2 us  [shards(): pl.pallas_call(functools.partial(kernel, nx, ny, nz), out_shape=jax.Shape...]
    another operation x4 -> x0, other arithmetic: 20.2 us -> none  [the longest x3 19.7 us: shards(): jax.scipy.linalg.solve_triangular(system, right, lower=True, unit_diagona...]
    dot_general x18 -> x0, matrix products: 12 us -> none  [the longest x3 4.62 us: shards(): jnp.dot(piece, weight, preferred_element_type=jnp.float32)]
    all_gather x1 -> x0, blocking collectives: 11.3 us -> none  [shards(): piece = lax.all_gather(tokens, 'head', axis=1, tiled=True)]
    unnamed x6 -> x17, local copies, waits for them, and re-layouts: 0.26 us -> 7.14 us
  transfers between devices with their start and end apart: 3 -> 0, of which waited for: 3 -> 0; matrix products, arithmetic and copies ran while one was open for 1% -> 0% of each run, Pallas kernels for 0% -> 0%
where the time goes in v1:
time: 74.7 us; the launch traced here: 74.4 us
  Pallas kernels  67.2 us (90%)
  local copies, waits for them, and re-layouts  7.14 us (10%)
    pallas_call x1, Pallas kernels, shards(): pl.pallas_call(functools.partial(kernel, nx, ny, nz), out_shape=jax.Shape...  67.2 us
    unnamed x17, local copies, waits for them, and re-layouts  7.14 us

profile of v1, /device:TPU:1, one launch (start us, length us, event | category | flops | bytes accessed | tf_op | source)
XLA Modules:
  0.0 74.4 jit_solution(11271845531249799546)
XLA Ops:
  0.0 0.0 copy-start.6
  0.0 0.0 copy-start.4
  0.0 0.7 copy-done.6
  0.7 0.1 copy.9.gate_ref
  0.8 0.0 copy-start.5
  0.8 0.8 %copy.10.beta_ref = s32[128,2]{1,0:T(8,128)S(1)} copy(s32[128,2]{0,1:T(2,128)} %param.13) | data formatting | bytes 2048 | tf_op args[5]
  1.6 0.0 copy-done.4
  1.6 0.0 copy-done.5
  1.6 0.0 copy-start
  1.6 1.2 %copy-done = bf16[2048,256]{1,0:T(8,128)(2,1)S(1)} copy-done((bf16[2048,256]{1,0:T(8,128)(2,1)S(1)}, bf16[2048,256]{1,0:T(8,128)(2,1)}, u32[]{:S(2)}) %copy-start) | copy-done | bytes 1048600
  2.8 0.0 copy-start.1
  2.8 1.2 %copy-done.1 = bf16[2048,256]{1,0:T(8,128)(2,1)S(1)} copy-done((bf16[2048,256]{1,0:T(8,128)(2,1)S(1)}, bf16[2048,256]{1,0:T(8,128)(2,1)}, u32[]{:S(2)}) %copy-start.1) | copy-done | bytes 1048600
  4.1 0.0 copy-start.2
  4.1 1.2 %copy-done.2 = bf16[2048,256]{1,0:T(8,128)(2,1)S(1)} copy-done((bf16[2048,256]{1,0:T(8,128)(2,1)S(1)}, bf16[2048,256]{1,0:T(8,128)(2,1)}, u32[]{:S(2)}) %copy-start.2) | copy-done | bytes 1048600
  5.3 0.0 copy-start.3
  5.3 1.2 %copy-done.3 = bf16[256,2048]{1,0:T(8,128)(2,1)S(1)} copy-done((bf16[256,2048]{1,0:T(8,128)(2,1)S(1)}, bf16[256,2048]{1,0:T(8,128)(2,1)}, u32[]{:S(2)}) %copy-start.3) | copy-done | bytes 1048600
  6.5 67.2 %shard_map.82 = bf16[128,512]{1,0:T(8,128)(2,1)S(1)} custom-call(bf16[128,512]{1,0:T(8,128)(2,1)S(1)} %copy-done.4, bf16[2048,256]{1,0:T(8,128)(2,1)S(1)} %copy-done, bf16[2048,256]{1,0:T(8,128)(2,1)S(1)} %copy-done.1, bf16[2048,256]{1,0:T(8,128)(2,1)S(1)} %copy-done.2, s32[128,2]{1,0:T(8,128)S(1)} %copy.9.gate_ref, s32[128,2]{1,0:T(8,128)S(1)} %copy.10.beta_ref, ...), custom_call_target="tpu_custom_call" | custom-call | tf_op jit(solution)/shard_map/pallas_call | solution.py:283
  73.7 0.7 copy.12
Async XLA Ops:
  0.0 0.7 copy-start.6
  0.0 1.6 %copy-start.4 = (bf16[128,512]{1,0:T(8,128)(2,1)S(1)}, bf16[128,512]{1,0:T(8,128)(2,1)}, u32[]{:S(2)}) copy-start(bf16[128,512]{1,0:T(8,128)(2,1)} %tok_ref.1) | copy-start | bytes 393220
  0.8 0.8 %copy-start.5 = (f32[128]{0:T(128)S(1)}, f32[128]{0:T(128)}, u32[]{:S(2)}) copy-start(f32[128]{0:T(128)} %param.14) | copy-start | bytes 1540
  1.6 1.2 %copy-start = (bf16[2048,256]{1,0:T(8,128)(2,1)S(1)}, bf16[2048,256]{1,0:T(8,128)(2,1)}, u32[]{:S(2)}) copy-start(bf16[2048,256]{1,0:T(8,128)(2,1)} %wq_hbm.1) | copy-start | bytes 3145732
  2.8 1.2 %copy-start.1 = (bf16[2048,256]{1,0:T(8,128)(2,1)S(1)}, bf16[2048,256]{1,0:T(8,128)(2,1)}, u32[]{:S(2)}) copy-start(bf16[2048,256]{1,0:T(8,128)(2,1)} %wk_hbm.1) | copy-start | bytes 3145732
  4.1 1.2 %copy-start.2 = (bf16[2048,256]{1,0:T(8,128)(2,1)S(1)}, bf16[2048,256]{1,0:T(8,128)(2,1)}, u32[]{:S(2)}) copy-start(bf16[2048,256]{1,0:T(8,128)(2,1)} %wv_hbm.1) | copy-start | bytes 3145732
  5.3 1.2 %copy-start.3 = (bf16[256,2048]{1,0:T(8,128)(2,1)S(1)}, bf16[256,2048]{1,0:T(8,128)(2,1)}, u32[]{:S(2)}) copy-start(bf16[256,2048]{1,0:T(8,128)(2,1)} %wo_hbm.1) | copy-start | bytes 3145732

commit v2 on v1

v2 whole, which is shorter than its diff:
```python
import functools
import jax
import jax.numpy as jnp
from jax import lax
from jax.experimental import pallas as pl
from jax.experimental.pallas import tpu as pltpu
from jax.sharding import PartitionSpec as P

MESH = pl.DeviceIdType.MESH
WIRE = jnp.bfloat16
F32 = jnp.float32
BF16 = jnp.bfloat16


def mm(a, b, dims=((1,), (0,))):
    return lax.dot_general(a, b, (dims, ((), ())), preferred_element_type=F32)


def halves(a):
    high = a.astype(BF16)
    return high, (a - high.astype(F32)).astype(BF16)


def dot3(a, b, dims=((1,), (0,))):
    a_high, a_low = halves(a)
    b_high, b_low = halves(b)
    return mm(a_high, b_high, dims) + (mm(a_high, b_low, dims) + mm(a_low, b_high, dims))


def dot2(a, b):
    a_high, a_low = halves(a)
    return mm(a_high, b) + mm(a_low, b)


def by_map(a, b):
    return dot2(a, b) if b.dtype == BF16 else dot3(a, b)


def below(top, rows):
    return jnp.concatenate([jnp.zeros((top, rows.shape[1]), F32), rows.astype(F32)], axis=0)


def unit_inverse(low, rows, cols):
    size = low.shape[0]
    eye = (rows == cols).astype(F32)
    base = jnp.where(rows // 8 == cols // 8, low, 0.0)
    square = dot3(base, base)
    fourth = dot3(square, square)
    result = dot3(dot3(eye - base, eye + square), eye + fourth)
    width = 8
    while width < size:
        mask = (rows // (2 * width) == cols // (2 * width)) & (rows // width > cols // width)
        corner = jnp.where(mask, low, 0.0)
        result = result - dot3(dot3(result, corner), result)
        width *= 2
    return result


def kernel(
    nx, ny, nz,
    tok_hbm, wq_hbm, wk_hbm, wv_hbm, gate_hbm, beta_hbm, gain_hbm, wo_hbm,
    out_ref,
    tok_all, wq, wk, wv, wo_all, gate_ref, beta_ref, gain_ref, ex_send, ex_recv, gz, gy, st_send, st_recv,
    norm_all, eff, intra,
    load_sem, x_send, x_recv, wo_send, wo_recv, n_send, n_recv, core_send, core_recv,
    z_send, z_recv, y_send, y_recv,
):
    index = lax.axis_index("seq")
    x = lax.axis_index("head")
    core = index % 2
    z = (index // 2) % nz
    y = index // (2 * nz)
    size = gain_ref.shape[1]
    n_tok, width = tok_hbm.shape
    out_cols = out_ref.shape[1]

    def at(y_to, z_to, core_to, x_to):
        return ((y_to * nz + z_to) * 2 + core_to, x_to)

    x_right, x_left = at(y, z, core, (x + 1) % nx), at(y, z, core, (x + nx - 1) % nx)
    z_right, z_left = at(y, (z + 1) % nz, core, x), at(y, (z + nz - 1) % nz, core, x)
    y_right, y_left = at((y + 1) % ny, z, core, x), at((y + ny - 1) % ny, z, core, x)
    partner = at(y, z, 1 - core, x)

    friends = [at(y, z, core, (x + d) % nx) for d in range(1, nx)]
    friends += [partner]
    friends += [z_right] + ([z_left] if nz > 2 else [])
    friends += [y_right] + ([y_left] if ny > 2 else [])
    barrier = pltpu.get_barrier_semaphore()
    for friend in friends:
        pl.semaphore_signal(barrier, inc=1, device_id=friend, device_id_type=MESH)

    own_cols = pl.ds(pl.multiple_of(x * out_cols, 128), out_cols)
    loads = [
        pltpu.make_async_copy(source, target, load_sem.at[i])
        for i, (source, target) in enumerate(
            (
                (tok_hbm, tok_all.at[x]), (gate_hbm, gate_ref), (beta_hbm, beta_ref), (wk_hbm, wk),
                (wv_hbm, wv), (wq_hbm, wq), (gain_hbm, gain_ref), (wo_hbm.at[:, own_cols], wo_all.at[x]),
            )
        )
    ]
    for load in loads:
        load.start()
    pl.semaphore_wait(barrier, len(friends))

    def send(source, target, s_sem, r_sem, to):
        return pltpu.make_async_remote_copy(
            src_ref=source, dst_ref=target, send_sem=s_sem, recv_sem=r_sem,
            device_id=to, device_id_type=MESH,
        )

    def x_gather(own, slots, s_sems, r_sems, use):
        half = own.shape[0] // 2
        before, after, across = (x + nx - 1) % nx, (x + 1) % nx, (x + 2) % nx
        first, second = [], []
        for k, part in enumerate((0, half)):
            other = half - part
            first.append(
                send(own.at[pl.ds(part, half)], slots.at[x, pl.ds(part, half)], s_sems.at[0, k], r_sems.at[0, k], x_right)
            )
            second.append(
                send(own.at[pl.ds(other, half)], slots.at[x, pl.ds(other, half)], s_sems.at[1, k], r_sems.at[1, k], x_left)
            )
            first[k].start()
            second[k].start()
        use(x, None)
        first[0].wait_recv()
        top = slots.at[before, pl.ds(0, half)]
        third = send(top, top, s_sems.at[2, 0], r_sems.at[2, 0], x_right)
        third.start()
        second[0].wait_recv()
        low = slots.at[after, pl.ds(half, half)]
        fourth = send(low, low, s_sems.at[3, 0], r_sems.at[3, 0], x_left)
        fourth.start()
        first[1].wait_recv()
        use(before, slots[before])
        second[1].wait_recv()
        use(after, slots[after])
        third.wait_recv()
        fourth.wait_recv()
        use(across, slots[across])
        return first + second + [third, fourth]

    rows = lax.broadcasted_iota(jnp.int32, (n_tok, n_tok), 0)
    cols = lax.broadcasted_iota(jnp.int32, (n_tok, n_tok), 1)
    lower = rows >= cols
    r2 = lax.broadcasted_iota(jnp.int32, (2 * size, size), 0)
    c2 = lax.broadcasted_iota(jnp.int32, (2 * size, size), 1)
    unit = (r2 == c2).astype(F32)
    heads = range(2)
    logs, incls, betas, lasts = [], [], [], []

    def gates():
        loads[1].wait()
        loads[2].wait()
        ones_up = (rows <= cols).astype(BF16)
        for head in heads:
            code = -gate_ref[head : head + 1, :].astype(F32) / 2097152.0
            beta = beta_ref[head : head + 1, :].astype(F32) / 256.0
            spread = jnp.broadcast_to(code, (n_tok, n_tok))
            c_high, c_low = halves(spread)
            c_last = (spread - c_high.astype(F32) - c_low.astype(F32)).astype(BF16)
            across = mm(c_high, ones_up) + (mm(c_low, ones_up) + mm(c_last, ones_up))
            log = across.T
            gaps = log - across
            logs.append(log)
            incls.append(jnp.where(lower, jnp.exp(jnp.where(lower, gaps, 0.0)), 0.0))
            betas.append(jnp.broadcast_to(beta, (n_tok, n_tok)).T)
            lasts.append(across[0:1, n_tok - 1 : n_tok])

    sums = [jnp.zeros((n_tok, wq.shape[1]), F32) for _ in range(2)]

    def project(place, block):
        if block is None:
            gates()
            loads[0].wait()
            loads[3].wait()
            loads[4].wait()
            block = tok_all[x]
        part = pl.ds(pl.multiple_of(place * width, 128), width)
        for i, weight in enumerate((wk, wv)):
            sums[i] = sums[i] + mm(block, weight[part, :])

    tok_copies = x_gather(tok_hbm, tok_all, x_send, x_recv, project)

    out_copies = []
    for d in range(1, nx):
        there = (x + d) % nx
        there_cols = pl.ds(pl.multiple_of(there * out_cols, 128), out_cols)
        out_copies.append(
            send(wo_hbm.at[:, there_cols], wo_all.at[x], wo_send.at[d - 1], wo_recv.at[d - 1],
                 at(y, z, core, there))
        )
    for copy in out_copies:
        copy.start()

    maps, keys, solves = [], [], []
    for head in heads:
        cut = slice(head * size, (head + 1) * size)
        key, value = (s[:, cut] for s in sums)
        key = key * lax.rsqrt(jnp.sum(key * key, -1, keepdims=True) + 1e-06)
        beta, log, last = betas[head], logs[head], lasts[head]
        low = jnp.where(rows > cols, beta * dot3(key, key, ((1,), (1,))) * incls[head], 0.0)
        inverse = unit_inverse(low, rows, cols)
        right = jnp.concatenate([beta * key * jnp.exp(log), beta * value], axis=1)
        solved = dot3(inverse, right)
        tail = key * jnp.exp(last - log)
        signed = jnp.concatenate([-solved[:, :size], solved[:, size:]], axis=1)
        moved = dot3(signed, tail, ((0,), (0,)))
        maps.append(moved + jnp.where(r2 == c2, jnp.exp(last), 0.0))
        keys.append(key)
        solves.append(solved)

    first_core = core == 0
    ex_send[...] = jnp.where(first_core, maps[1], maps[0])
    swap = send(ex_send, ex_recv, core_send.at[0], core_recv.at[0], partner)
    swap.start()
    mine = jnp.where(first_core, maps[0], maps[1])
    swap.wait_recv()
    other = ex_recv[...]
    early = jnp.where(first_core, mine, other)
    late = jnp.where(first_core, other, mine)
    gz[z] = (dot3(early, late[:size]) + below(size, late[size:])).astype(WIRE)

    def ring(slots, place, count, s_sems, r_sems, to, fill):
        chunks = r_sems.shape[2]
        rows_each = slots.shape[1] // chunks
        far = count // 2
        sent = []
        waiting = {}
        for step in range(far):
            for chunk in range(chunks):
                for way in range(2):
                    if step == far - 1 and (chunk < chunks // 2) != (way == 0):
                        continue
                    if step:
                        waiting.pop((way, step - 1, chunk)).wait_recv()
                    slot = (place + count - step) % count if way == 0 else (place + step) % count
                    piece = slots.at[slot, pl.ds(chunk * rows_each, rows_each)]
                    copy = send(piece, piece, s_sems.at[way, step, chunk], r_sems.at[way, step, chunk], to[way])
                    copy.start()
                    sent.append(copy)
                    waiting[way, step, chunk] = copy
            if step < len(fill):
                fill[step]()
        for copy in waiting.values():
            copy.wait_recv()
        return sent

    queries = []

    def ask():
        loads[5].wait()
        total = jnp.zeros((n_tok, wq.shape[1]), F32)
        for place in range(nx):
            total = total + mm(tok_all[place], wq[place * width : (place + 1) * width, :])
        queries.append(total)

    def inside(head):
        query = queries[0][:, head * size : (head + 1) * size]
        dots = dot3(query, keys[head], ((1,), (1,))) * incls[head]
        inner = dot3(dots, solves[head])
        intra[head] = inner[:, size:]
        eff[head] = query * jnp.exp(logs[head]) - inner[:, :size]

    def join(left, right):
        return by_map(left, right[:size]) + below(size, right[size:])

    def pairs(slots, count):
        levels = [[slots[j] for j in range(count)]]
        while len(levels[-1]) > 1:
            level = [part.astype(F32) for part in levels[-1]]
            levels.append([join(level[j], levels[-1][j + 1]) for j in range(0, len(level), 2)])
        return levels

    def pieces(levels, place):
        found = []
        for depth in reversed(range(len(levels) - 1)):
            step = 2 ** depth
            bit = (place // step) % 2 == 1
            chosen = levels[depth][0].astype(F32)
            for j in range(2, len(levels[depth]), 2):
                chosen = jnp.where(place // (2 * step) == j // 2, levels[depth][j].astype(F32), chosen)
            found.append(jnp.where(bit, chosen, unit))
        return found

    z_copies = ring(
        gz, z, nz, z_send, z_recv, (z_right, z_left),
        [ask, functools.partial(inside, 0), functools.partial(inside, 1)][: nz // 2],
    )
    if nz // 2 < 3:
        for late_work in [ask, functools.partial(inside, 0), functools.partial(inside, 1)][nz // 2 :]:
            late_work()
    levels = pairs(gz, nz)
    gy[y] = levels[-1][0].astype(WIRE)
    prefix = []

    def before_here():
        found = pieces(levels, z)
        total = found[0]
        for part in found[1:]:
            total = dot3(total, part[:size]) + below(size, part[size:])
        prefix.append(total)

    y_copies = ring(gy, y, ny, y_send, y_recv, (y_right, y_left), [before_here])
    found = pieces(pairs(gy, ny), y)
    state = found[0][size:]
    for part in found[1:] + prefix:
        state = dot3(state, part[:size]) + part[size:]
    chip = state
    second = dot3(chip, early[:size]) + early[size:]
    st_send[...] = jnp.where(first_core, second, chip)
    give = send(st_send, st_recv, core_send.at[1], core_recv.at[1], partner)
    give.start()
    kept = jnp.where(first_core, chip, second)
    loads[6].wait()
    loads[7].wait()
    give.wait_recv()
    got = st_recv[...]
    states = [jnp.where(first_core, kept, got), jnp.where(first_core, got, kept)]
    gain = gain_ref[...]
    for head in heads:
        o = intra[head] + dot3(eff[head], states[head], ((1,), (1,)))
        scale = lax.rsqrt(jnp.mean(o * o, -1, keepdims=True) + 1e-06)
        norm_all[x, :, head * size : (head + 1) * size] = (o * scale * gain).astype(BF16)

    result = [jnp.zeros((n_tok, out_cols), F32)]

    def finish(place, block):
        if block is None:
            for copy in out_copies:
                copy.wait_recv()
            block = norm_all[x]
        result[0] = result[0] + mm(block, wo_all[place])

    n_copies = x_gather(norm_all.at[x], norm_all, n_send, n_recv, finish)
    out_ref[...] = result[0].astype(BF16)
    for copy in tok_copies + out_copies + z_copies + y_copies + [swap, give] + n_copies:
        copy.wait_send()


def shards(ny, nz, nx, tokens, w_query, w_key, w_value, gate_codes, beta_codes, norm_gain, w_out):
    n_tok, width = tokens.shape
    size = norm_gain.shape[0]
    here = w_query.shape[1]
    hbm = pl.BlockSpec(memory_space=pltpu.HBM)
    chunks = 4
    dma = pltpu.SemaphoreType.DMA
    return pl.pallas_call(
        functools.partial(kernel, nx, ny, nz),
        out_shape=jax.ShapeDtypeStruct((n_tok, w_out.shape[1] // nx), BF16),
        in_specs=[hbm] * 8,
        out_specs=pl.BlockSpec(memory_space=pltpu.VMEM),
        scratch_shapes=[
            pltpu.VMEM((nx, n_tok, width), BF16),
            pltpu.VMEM(w_query.shape, BF16),
            pltpu.VMEM(w_key.shape, BF16),
            pltpu.VMEM(w_value.shape, BF16),
            pltpu.VMEM((nx, here, w_out.shape[1] // nx), BF16),
            pltpu.VMEM((2, n_tok), jnp.int32),
            pltpu.VMEM((2, n_tok), jnp.int32),
            pltpu.VMEM((1, size), F32),
            pltpu.VMEM((2 * size, size), F32),
            pltpu.VMEM((2 * size, size), F32),
            pltpu.VMEM((nz, 2 * size, size), WIRE),
            pltpu.VMEM((ny, 2 * size, size), WIRE),
            pltpu.VMEM((size, size), F32),
            pltpu.VMEM((size, size), F32),
            pltpu.VMEM((nx, n_tok, here), BF16),
            pltpu.VMEM((2, n_tok, size), F32),
            pltpu.VMEM((2, n_tok, size), F32),
            dma((8,)), dma((4, 2)), dma((4, 2)), dma((nx - 1,)), dma((nx - 1,)), dma((4, 2)), dma((4, 2)),
            dma((2,)), dma((2,)), dma((2, nz, chunks)), dma((2, nz, chunks)), dma((2, ny, chunks)),
            dma((2, ny, chunks)),
        ],
        compiler_params=pltpu.CompilerParams(
            collective_id=0, has_side_effects=True, vmem_limit_bytes=67043328
        ),
    )(tokens, w_query, w_key, w_value, gate_codes.T, beta_codes.T, norm_gain.reshape(1, size), w_out)


def solution(mesh):
    chips = mesh.shape["seq"] // 2
    nz = 1
    while nz * nz < chips:
        nz *= 2
    return jax.shard_map(
        functools.partial(shards, chips // nz, nz, mesh.shape["head"]),
        mesh=mesh,
        in_specs=(
            P("seq", "head"), P(None, "head"), P(None, "head"), P(None, "head"),
            P("seq", "head"), P("seq", "head"), P(), P("head", None),
        ),
        out_specs=P("seq", "head"),
        check_vma=False,
    )
```

time: 74.7 us -> 66.6 us (0.89)
  local copies, waits for them, and re-layouts: 7.14 us -> 1.57 us
  Pallas kernels: 67.2 us -> 64.9 us
    unnamed x17 -> x1, local copies, waits for them, and re-layouts: 7.14 us -> 1.57 us
    pallas_call x1, Pallas kernels: 67.2 us -> 64.9 us  [shards(): pl.pallas_call(functools.partial(kernel, nx, ny, nz), out_shape=jax.Shape...]
where the time goes in v2:
time: 66.6 us; the launch traced here: 66.4 us
  Pallas kernels  64.9 us (97%)
  local copies, waits for them, and re-layouts  1.57 us (2%)
    pallas_call x1, Pallas kernels, shards(): pl.pallas_call(functools.partial(kernel, nx, ny, nz), out_shape=jax.Shape...  64.9 us
    unnamed x1, local copies, waits for them, and re-layouts  1.57 us

profile of v2, /device:TPU:1, one launch (start us, length us, event | category | flops | bytes accessed | tf_op | source)
XLA Modules:
  0.0 66.4 jit_solution(11829769723850072560)
XLA Ops:
  0.0 64.9 %shard_map.82 = bf16[128,512]{1,0:T(8,128)(2,1)} custom-call(bf16[128,512]{1,0:T(8,128)(2,1)} %tok_hbm.1, bf16[2048,256]{1,0:T(8,128)(2,1)} %wq_hbm.1, bf16[2048,256]{1,0:T(8,128)(2,1)} %wk_hbm.1, bf16[2048,256]{1,0:T(8,128)(2,1)} %wv_hbm.1, s32[2,128]{1,0:T(2,128)} %bitcast.3, s32[2,128]{1,0:T(2,128)} %bitcast.4, f32[1,128]{1,0:T(1,128)} %bitcast.5, ...), custom_call_target="tpu_custom_call" | custom-call | tf_op jit(solution)/shard_map/pallas_call | solution.py:350
  64.9 1.6 %copy.10 = bf16[128,512]{1,0:T(8,128)(2,1)} copy(bf16[128,512]{1,0:T(8,128)(2,1)} %shard_map.82) | data formatting | bytes 262144

commit v3 on v2

--- a/solution.py
+++ b/solution.py
@@ -74,18 +74,24 @@
     n_tok, width = tok_hbm.shape
     out_cols = out_ref.shape[1]
 
-    def at(y_to, z_to, core_to, x_to):
-        return ((y_to * nz + z_to) * 2 + core_to, x_to)
+    def at(to_y, to_z, to_core, to_x):
+        return ((to_y * nz + to_z) * 2 + to_core, to_x)
 
     x_right, x_left = at(y, z, core, (x + 1) % nx), at(y, z, core, (x + nx - 1) % nx)
-    z_right, z_left = at(y, (z + 1) % nz, core, x), at(y, (z + nz - 1) % nz, core, x)
-    y_right, y_left = at((y + 1) % ny, z, core, x), at((y + ny - 1) % ny, z, core, x)
+
+    def z_to(d):
+        return at(y, (z + d + nz) % nz, core, x)
+
+    def y_to(d):
+        return at((y + d + ny) % ny, z, core, x)
+
     partner = at(y, z, 1 - core, x)
 
     friends = [at(y, z, core, (x + d) % nx) for d in range(1, nx)]
     friends += [partner]
-    friends += [z_right] + ([z_left] if nz > 2 else [])
-    friends += [y_right] + ([y_left] if ny > 2 else [])
+    for count, toward in ((nz, z_to), (ny, y_to)):
+        steps = {d % count for d in ((1, -1, 2, -2) if count == 8 else (1, -1))} - {0}
+        friends += [toward(d) for d in sorted(steps)]
     barrier = pltpu.get_barrier_semaphore()
     for friend in friends:
         pl.semaphore_signal(barrier, inc=1, device_id=friend, device_id_type=MESH)
@@ -223,7 +229,45 @@
     late = jnp.where(first_core, other, mine)
     gz[z] = (dot3(early, late[:size]) + below(size, late[size:])).astype(WIRE)
 
+    def ring_of_eight(slots, place, s_sems, r_sems, to, fill):
+        chunks = r_sems.shape[2]
+        rows_each = slots.shape[1] // chunks
+        copies = {}
+
+        def go(way, distance, chunk, hops):
+            sign = 1 - 2 * way
+            slot = (place - sign * (distance - hops) + 8) % 8
+            piece = slots.at[slot, pl.ds(chunk * rows_each, rows_each)]
+            copy = send(
+                piece, piece, s_sems.at[way, distance - 1, chunk], r_sems.at[way, distance - 1, chunk], to(sign * hops)
+            )
+            copy.start()
+            copies[way, distance, chunk] = copy
+
+        order = list(range(chunks))
+        turns = (order, order[::-1])
+        for distance in (2, 1):
+            for k in order:
+                for way in range(2):
+                    go(way, distance, turns[way][k], distance)
+        fill[0]()
+        for k in order:
+            for way in range(2):
+                chunk = turns[way][k]
+                copies[way, 2, chunk].wait_recv()
+                if k < chunks // 2:
+                    go(way, 4, chunk, 2)
+                go(way, 3, chunk, 1)
+        for work in fill[1:]:
+            work()
+        for (way, distance, chunk), copy in copies.items():
+            if distance != 2:
+                copy.wait_recv()
+        return list(copies.values())
+
     def ring(slots, place, count, s_sems, r_sems, to, fill):
+        if count == 8:
+            return ring_of_eight(slots, place, s_sems, r_sems, to, fill)
         chunks = r_sems.shape[2]
         rows_each = slots.shape[1] // chunks
         far = count // 2
@@ -238,7 +282,9 @@
                         waiting.pop((way, step - 1, chunk)).wait_recv()
                     slot = (place + count - step) % count if way == 0 else (place + step) % count
                     piece = slots.at[slot, pl.ds(chunk * rows_each, rows_each)]
-                    copy = send(piece, piece, s_sems.at[way, step, chunk], r_sems.at[way, step, chunk], to[way])
+                    copy = send(
+                        piece, piece, s_sems.at[way, step, chunk], r_sems.at[way, step, chunk], to(1 - 2 * way)
+                    )
                     copy.start()
                     sent.append(copy)
                     waiting[way, step, chunk] = copy
@@ -285,13 +331,11 @@
             found.append(jnp.where(bit, chosen, unit))
         return found
 
-    z_copies = ring(
-        gz, z, nz, z_send, z_recv, (z_right, z_left),
-        [ask, functools.partial(inside, 0), functools.partial(inside, 1)][: nz // 2],
-    )
-    if nz // 2 < 3:
-        for late_work in [ask, functools.partial(inside, 0), functools.partial(inside, 1)][nz // 2 :]:
-            late_work()
+    def rest():
+        for head in heads:
+            inside(head)
+
+    z_copies = ring(gz, z, nz, z_send, z_recv, z_to, [ask, rest])
     levels = pairs(gz, nz)
     gy[y] = levels[-1][0].astype(WIRE)
     prefix = []
@@ -303,7 +347,7 @@
             total = dot3(total, part[:size]) + below(size, part[size:])
         prefix.append(total)
 
-    y_copies = ring(gy, y, ny, y_send, y_recv, (y_right, y_left), [before_here])
+    y_copies = ring(gy, y, ny, y_send, y_recv, y_to, [before_here])
     found = pieces(pairs(gy, ny), y)
     state = found[0][size:]
     for part in found[1:] + prefix:
@@ -345,7 +389,7 @@
     size = norm_gain.shape[0]
     here = w_query.shape[1]
     hbm = pl.BlockSpec(memory_space=pltpu.HBM)
-    chunks = 4
+    chunks = 2
     dma = pltpu.SemaphoreType.DMA
     return pl.pallas_call(
         functools.partial(kernel, nx, ny, nz),
@@ -380,11 +424,16 @@
     )(tokens, w_query, w_key, w_value, gate_codes.T, beta_codes.T, norm_gain.reshape(1, size), w_out)
 
 
-def solution(mesh):
-    chips = mesh.shape["seq"] // 2
+def along_z(chips):
     nz = 1
     while nz * nz < chips:
         nz *= 2
+    return nz
+
+
+def solution(mesh):
+    chips = mesh.shape["seq"] // 2
+    nz = along_z(chips)
     return jax.shard_map(
         functools.partial(shards, chips // nz, nz, mesh.shape["head"]),
         mesh=mesh,

time: 66.6 us -> 59.9 us (0.90)
  Pallas kernels: 64.9 us -> 58.2 us
    pallas_call x1, Pallas kernels: 64.9 us -> 58.2 us  [shards(): pl.pallas_call(functools.partial(kernel, nx, ny, nz), out_shape=jax.Shape...]
where the time goes in v3:
time: 59.9 us; the launch traced here: 59.8 us
  Pallas kernels  58.2 us (97%)
  local copies, waits for them, and re-layouts  1.57 us (3%)
    pallas_call x1, Pallas kernels, shards(): pl.pallas_call(functools.partial(kernel, nx, ny, nz), out_shape=jax.Shape...  58.2 us
    unnamed x1, local copies, waits for them, and re-layouts  1.57 us

profile of v3, /device:TPU:1, one launch (start us, length us, event | category | flops | bytes accessed | tf_op | source)
XLA Modules:
  0.0 59.8 jit_solution(15167205496594936579)
XLA Ops:
  0.0 58.2 %shard_map.82 = bf16[128,512]{1,0:T(8,128)(2,1)} custom-call(bf16[128,512]{1,0:T(8,128)(2,1)} %tok_hbm.1, bf16[2048,256]{1,0:T(8,128)(2,1)} %wq_hbm.1, bf16[2048,256]{1,0:T(8,128)(2,1)} %wk_hbm.1, bf16[2048,256]{1,0:T(8,128)(2,1)} %wv_hbm.1, s32[2,128]{1,0:T(2,128)} %bitcast.3, s32[2,128]{1,0:T(2,128)} %bitcast.4, f32[1,128]{1,0:T(1,128)} %bitcast.5, ...), custom_call_target="tpu_custom_call" | custom-call | tf_op jit(solution)/shard_map/pallas_call | solution.py:394
  58.2 1.6 %copy.10 = bf16[128,512]{1,0:T(8,128)(2,1)} copy(bf16[128,512]{1,0:T(8,128)(2,1)} %shard_map.82) | data formatting | bytes 262144

commit v4 on v3

--- a/solution.py
+++ b/solution.py
@@ -24,7 +24,10 @@
 def dot3(a, b, dims=((1,), (0,))):
     a_high, a_low = halves(a)
     b_high, b_low = halves(b)
-    return mm(a_high, b_high, dims) + (mm(a_high, b_low, dims) + mm(a_low, b_high, dims))
+    free = 1 - dims[1][0]
+    count = b.shape[free]
+    both = mm(a_high, jnp.concatenate([b_high, b_low], axis=free), dims)
+    return both[:, :count] + (both[:, count:] + mm(a_low, b_high, dims))
 
 
 def dot2(a, b):
@@ -92,6 +95,7 @@
     for count, toward in ((nz, z_to), (ny, y_to)):
         steps = {d % count for d in ((1, -1, 2, -2) if count == 8 else (1, -1))} - {0}
         friends += [toward(d) for d in sorted(steps)]
+    gy[...] = jnp.zeros(gy.shape, WIRE)
     barrier = pltpu.get_barrier_semaphore()
     for friend in friends:
         pl.semaphore_signal(barrier, inc=1, device_id=friend, device_id_type=MESH)
@@ -229,10 +233,17 @@
     late = jnp.where(first_core, other, mine)
     gz[z] = (dot3(early, late[:size]) + below(size, late[size:])).astype(WIRE)
 
-    def ring_of_eight(slots, place, s_sems, r_sems, to, fill):
+    def ring_of_eight(slots, place, s_sems, r_sems, to, fill, earlier_only):
         chunks = r_sems.shape[2]
         rows_each = slots.shape[1] // chunks
         copies = {}
+
+        def wanted(way, distance, source, act):
+            if earlier_only:
+                limit = 8 - distance if way == 0 else (1, 4, 3, 4)[distance - 1]
+                pl.when(source < limit)(act)
+            else:
+                act()
 
         def go(way, distance, chunk, hops):
             sign = 1 - 2 * way
@@ -241,8 +252,12 @@
             copy = send(
                 piece, piece, s_sems.at[way, distance - 1, chunk], r_sems.at[way, distance - 1, chunk], to(sign * hops)
             )
-            copy.start()
-            copies[way, distance, chunk] = copy
+            wanted(way, distance, slot, copy.start)
+            copies[way, distance, chunk] = copy, slot
+
+        def arrive(way, distance, chunk):
+            source = (place - (1 - 2 * way) * distance + 8) % 8
+            wanted(way, distance, source, copies[way, distance, chunk][0].wait_recv)
 
         order = list(range(chunks))
         turns = (order, order[::-1])
@@ -254,20 +269,24 @@
         for k in order:
             for way in range(2):
                 chunk = turns[way][k]
-                copies[way, 2, chunk].wait_recv()
-                if k < chunks // 2:
+                arrive(way, 2, chunk)
+                if way == 1 if earlier_only else k < chunks // 2:
                     go(way, 4, chunk, 2)
                 go(way, 3, chunk, 1)
         for work in fill[1:]:
             work()
-        for (way, distance, chunk), copy in copies.items():
+        for way, distance, chunk in copies:
             if distance != 2:
-                copy.wait_recv()
-        return list(copies.values())
-
-    def ring(slots, place, count, s_sems, r_sems, to, fill):
+                arrive(way, distance, chunk)
+
+        def left(way, distance, copy, slot):
+            wanted(way, distance, slot, copy.wait_send)
+
+        return [functools.partial(left, way, distance, *copy) for (way, distance, _), copy in copies.items()]
+
+    def ring(slots, place, count, s_sems, r_sems, to, fill, earlier_only=False):
         if count == 8:
-            return ring_of_eight(slots, place, s_sems, r_sems, to, fill)
+            return ring_of_eight(slots, place, s_sems, r_sems, to, fill, earlier_only)
         chunks = r_sems.shape[2]
         rows_each = slots.shape[1] // chunks
         far = count // 2
@@ -290,9 +309,11 @@
                     waiting[way, step, chunk] = copy
             if step < len(fill):
                 fill[step]()
+        for work in fill[far:]:
+            work()
         for copy in waiting.values():
             copy.wait_recv()
-        return sent
+        return [copy.wait_send for copy in sent]
 
     queries = []
 
@@ -347,7 +368,7 @@
             total = dot3(total, part[:size]) + below(size, part[size:])
         prefix.append(total)
 
-    y_copies = ring(gy, y, ny, y_send, y_recv, y_to, [before_here])
+    y_copies = ring(gy, y, ny, y_send, y_recv, y_to, [before_here], True)
     found = pieces(pairs(gy, ny), y)
     state = found[0][size:]
     for part in found[1:] + prefix:
@@ -380,8 +401,10 @@
 
     n_copies = x_gather(norm_all.at[x], norm_all, n_send, n_recv, finish)
     out_ref[...] = result[0].astype(BF16)
-    for copy in tok_copies + out_copies + z_copies + y_copies + [swap, give] + n_copies:
+    for copy in tok_copies + out_copies + [swap, give] + n_copies:
         copy.wait_send()
+    for finished in z_copies + y_copies:
+        finished()
 
 
 def shards(ny, nz, nx, tokens, w_query, w_key, w_value, gate_codes, beta_codes, norm_gain, w_out):

time: 59.9 us -> 59 us (0.985)
  the two profiles are of different devices: /device:TPU:1 before, /device:TPU:58 now
where the time goes in v4:
time: 59 us; the launch traced here: 58.9 us
  Pallas kernels  57.3 us (97%)
  local copies, waits for them, and re-layouts  1.57 us (3%)
    pallas_call x1, Pallas kernels, shards(): pl.pallas_call(functools.partial(kernel, nx, ny, nz), out_shape=jax.Shape...  57.3 us
    unnamed x1, local copies, waits for them, and re-layouts  1.57 us

profile of v4, /device:TPU:58, one launch (start us, length us, event | category | flops | bytes accessed | tf_op | source)
XLA Modules:
  0.0 58.9 jit_solution(2015396332697280736)
XLA Ops:
  0.0 57.3 %shard_map.82 = bf16[128,512]{1,0:T(8,128)(2,1)} custom-call(bf16[128,512]{1,0:T(8,128)(2,1)} %tok_hbm.1, bf16[2048,256]{1,0:T(8,128)(2,1)} %wq_hbm.1, bf16[2048,256]{1,0:T(8,128)(2,1)} %wk_hbm.1, bf16[2048,256]{1,0:T(8,128)(2,1)} %wv_hbm.1, s32[2,128]{1,0:T(2,128)} %bitcast.3, s32[2,128]{1,0:T(2,128)} %bitcast.4, f32[1,128]{1,0:T(1,128)} %bitcast.5, ...), custom_call_target="tpu_custom_call" | custom-call | tf_op jit(solution)/shard_map/pallas_call | solution.py:417
  57.3 1.6 %copy.10 = bf16[128,512]{1,0:T(8,128)(2,1)} copy(bf16[128,512]{1,0:T(8,128)(2,1)} %shard_map.82) | data formatting | bytes 262144

commit v5 on v3

--- a/solution.py
+++ b/solution.py
@@ -24,7 +24,10 @@
 def dot3(a, b, dims=((1,), (0,))):
     a_high, a_low = halves(a)
     b_high, b_low = halves(b)
-    return mm(a_high, b_high, dims) + (mm(a_high, b_low, dims) + mm(a_low, b_high, dims))
+    free = 1 - dims[1][0]
+    count = b.shape[free]
+    both = mm(a_high, jnp.concatenate([b_high, b_low], axis=free), dims)
+    return both[:, :count] + (both[:, count:] + mm(a_low, b_high, dims))
 
 
 def dot2(a, b):
@@ -290,6 +293,8 @@
                     waiting[way, step, chunk] = copy
             if step < len(fill):
                 fill[step]()
+        for work in fill[far:]:
+            work()
         for copy in waiting.values():
             copy.wait_recv()
         return sent

time: 59.9 us -> 59.2 us (0.988)
  Pallas kernels: 58.2 us -> 57.5 us
    pallas_call x1, Pallas kernels: 58.2 us -> 57.5 us  [shards(): pl.pallas_call(functools.partial(kernel, nx, ny, nz), out_shape=jax.Shape...]
where the time goes in v5:
time: 59.2 us; the launch traced here: 59 us
  Pallas kernels  57.5 us (97%)
  local copies, waits for them, and re-layouts  1.57 us (3%)
    pallas_call x1, Pallas kernels, shards(): pl.pallas_call(functools.partial(kernel, nx, ny, nz), out_shape=jax.Shape...  57.5 us
    unnamed x1, local copies, waits for them, and re-layouts  1.57 us

profile of v5, /device:TPU:1, one launch (start us, length us, event | category | flops | bytes accessed | tf_op | source)
XLA Modules:
  0.0 59.0 jit_solution(153491110454900285)
XLA Ops:
  0.0 57.5 %shard_map.82 = bf16[128,512]{1,0:T(8,128)(2,1)} custom-call(bf16[128,512]{1,0:T(8,128)(2,1)} %tok_hbm.1, bf16[2048,256]{1,0:T(8,128)(2,1)} %wq_hbm.1, bf16[2048,256]{1,0:T(8,128)(2,1)} %wk_hbm.1, bf16[2048,256]{1,0:T(8,128)(2,1)} %wv_hbm.1, s32[2,128]{1,0:T(2,128)} %bitcast.3, s32[2,128]{1,0:T(2,128)} %bitcast.4, f32[1,128]{1,0:T(1,128)} %bitcast.5, ...), custom_call_target="tpu_custom_call" | custom-call | tf_op jit(solution)/shard_map/pallas_call | solution.py:399
  57.5 1.6 %copy.10 = bf16[128,512]{1,0:T(8,128)(2,1)} copy(bf16[128,512]{1,0:T(8,128)(2,1)} %shard_map.82) | data formatting | bytes 262144

commit v6 on v5

--- a/solution.py
+++ b/solution.py
@@ -201,8 +201,6 @@
             send(wo_hbm.at[:, there_cols], wo_all.at[x], wo_send.at[d - 1], wo_recv.at[d - 1],
                  at(y, z, core, there))
         )
-    for copy in out_copies:
-        copy.start()
 
     maps, keys, solves = [], [], []
     for head in heads:
@@ -225,6 +223,8 @@
     ex_send[...] = jnp.where(first_core, maps[1], maps[0])
     swap = send(ex_send, ex_recv, core_send.at[0], core_recv.at[0], partner)
     swap.start()
+    for copy in out_copies:
+        copy.start()
     mine = jnp.where(first_core, maps[0], maps[1])
     swap.wait_recv()
     other = ex_recv[...]

time: 59.2 us -> 59.2 us (level)
  no operation moved by 1% of the time
where the time goes in v6:
time: 59.2 us; the launch traced here: 59 us
  Pallas kernels  57.4 us (97%)
  local copies, waits for them, and re-layouts  1.57 us (3%)
    pallas_call x1, Pallas kernels, shards(): pl.pallas_call(functools.partial(kernel, nx, ny, nz), out_shape=jax.Shape...  57.4 us
    unnamed x1, local copies, waits for them, and re-layouts  1.57 us

profile of v6, /device:TPU:1, one launch (start us, length us, event | category | flops | bytes accessed | tf_op | source)
XLA Modules:
  0.0 59.0 jit_solution(10197006735812259300)
XLA Ops:
  0.0 57.4 %shard_map.82 = bf16[128,512]{1,0:T(8,128)(2,1)} custom-call(bf16[128,512]{1,0:T(8,128)(2,1)} %tok_hbm.1, bf16[2048,256]{1,0:T(8,128)(2,1)} %wq_hbm.1, bf16[2048,256]{1,0:T(8,128)(2,1)} %wk_hbm.1, bf16[2048,256]{1,0:T(8,128)(2,1)} %wv_hbm.1, s32[2,128]{1,0:T(2,128)} %bitcast.3, s32[2,128]{1,0:T(2,128)} %bitcast.4, f32[1,128]{1,0:T(1,128)} %bitcast.5, ...), custom_call_target="tpu_custom_call" | custom-call | tf_op jit(solution)/shard_map/pallas_call | solution.py:399
  57.5 1.6 %copy.10 = bf16[128,512]{1,0:T(8,128)(2,1)} copy(bf16[128,512]{1,0:T(8,128)(2,1)} %shard_map.82) | data formatting | bytes 262144
